TPU v7x, 128 devices: a whole 4x4x4 slice. The times are simulated.
128 devices in a mesh: expert: 4 (over z), panel: 32 (over y, x, core).
Axes of the slice: x: 4, y: 4, z: 4, core: 2. Of those that a mesh axis runs over, the one named last changes fastest.
Arguments:
- tokens: bfloat16 [4096, 6144], P(('expert', 'panel')), may hold values from -6 to 6
- routes: int32 [4096, 2], P(('expert', 'panel')), may hold values from 0 to 7, all different within a row; in each aligned block of 32 rows (0 to 31, 32 to 63, ...) at most 12 rows name the same one
- router_weights: float32 [4096, 2], P(('expert', 'panel')), may hold values from 0.05 to 0.95
Outputs:
- hessian: float32 [8, 6144, 6144], P('expert', 'panel')
Inputs may be any that keep to these rules, and one draw needn't show every extreme that they name: `routes`: each row names two different experts; among the 32 rows of one device no expert is named more than 12 times, a bound that some block reaches.
All inputs are finite; a program needn't handle non-finite values.
Results may differ from a plain program's by a relative error of at most 0.0036.
Values may be sent and summed in bfloat16 or wider, within the bound.
A program may use at most 192 MiB of HBM per device.

v0:
```python
import jax
import jax.numpy as jnp
from jax import lax
from jax.sharding import PartitionSpec as P

EXP_DEV = 2
CAP = 12


def per_device(tokens, routes, router_weights):
    tok_count = tokens.shape[0]
    width = tokens.shape[1]
    groups = lax.axis_size("expert")
    panels = lax.axis_size("panel")
    experts_all = EXP_DEV * groups
    slot_count = experts_all * CAP
    flat = routes.reshape(-1)
    onehot = (flat[:, None] == jnp.arange(experts_all, dtype=jnp.int32)[None, :]).astype(jnp.int32)
    before = jnp.cumsum(onehot, axis=0) - onehot
    places = flat * CAP + jnp.sum(onehot * before, axis=1)
    placing = (places[None, :] == jnp.arange(slot_count, dtype=jnp.int32)[:, None]).astype(
        jnp.float32
    )
    placing = placing.reshape(slot_count, tok_count, 2)
    picker = (placing[:, :, 0] + placing[:, :, 1]).astype(jnp.bfloat16)
    routed_rows = jnp.dot(picker, tokens, preferred_element_type=jnp.float32).astype(jnp.bfloat16)
    rounded = router_weights.astype(jnp.bfloat16).astype(jnp.float32)
    routed_weights = jnp.einsum(
        "jtk,tk->j", placing, rounded, precision=lax.Precision.HIGHEST
    ).astype(jnp.bfloat16)
    routed_rows = routed_rows.reshape(groups, EXP_DEV * CAP, width)
    routed_weights = routed_weights.reshape(groups, EXP_DEV * CAP)
    panel_index = lax.axis_index("panel")
    panel_width = width // panels
    scaling = float(groups * panels * CAP) ** (-0.5)
    arrived_rows, arrived_weights = (
        lax.all_to_all(routed_rows, "expert", split_axis=0, concat_axis=0, tiled=True),
        lax.all_to_all(routed_weights, "expert", split_axis=0, concat_axis=0, tiled=True),
    )
    rows_four = lax.all_gather(arrived_rows, "panel", axis=0, tiled=True).reshape(
        -1, EXP_DEV, CAP, width
    )
    weights_four = lax.all_gather(arrived_weights, "panel", axis=0, tiled=True).reshape(
        -1, EXP_DEV, CAP
    )
    columns = lax.dynamic_slice_in_dim(rows_four, panel_index * panel_width, panel_width, 3)
    scaled = (weights_four[..., None].astype(jnp.float32) * rows_four.astype(jnp.float32)).astype(
        jnp.bfloat16
    )
    totals = jnp.einsum("secu,secd->eud", columns, scaled, preferred_element_type=jnp.float32)
    return totals * scaling


def solution(mesh):
    placed = (
        P(("expert", "panel"), None),
        P(("expert", "panel"), None),
        P(("expert", "panel"), None),
    )
    return jax.shard_map(
        per_device,
        mesh=mesh,
        in_specs=placed,
        out_specs=P("expert", "panel", None),
        check_vma=False,
    )
```

profile of v0, /device:TPU:1, one launch (start us, length us, event | category | flops | bytes accessed | tf_op | source)
XLA Modules:
  0.0 232.9 jit_solution(14246586715702602953)
XLA Ops:
  6.5 0.0 copy-start
  6.5 0.0 all-gather.3.cloned.1.call-start
  6.5 0.8 copy.25
  7.3 0.1 eq.30
  7.5 0.1 fusion.5
  7.5 0.1 reduce_window_sum.11
  7.6 0.2 select_reduce_fusion
  7.8 0.1 reduce_sum.12
  7.9 0.1 copy.26
  8.0 0.7 multiply_add_fusion
  8.7 0.1 fusion.4
  8.8 0.0 copy-done
  8.8 0.5 convolution_convert_fusion
  9.3 21.3 %all_to_all.18 = bf16[4,24,6144]{2,1,0:T(8,128)(2,1)} all-to-all(bf16[4,24,6144]{2,1,0:T(8,128)(2,1)S(1)} %bitcast.18), channel_id=1, replica_groups=mesh['expert'=4,'panel'=32] {'expert'}, dimensions={0} | all-to-all | bytes 2359296 | tf_op jit(solution)/shard_map/all_to_all | solution.py:37
  30.6 0.0 all-gather.3.cloned.1.call-update
  30.6 0.7 convert_bitcast_fusion
  31.3 0.2 fusion.3
  31.5 0.7 all_to_all.15
  32.2 3.2 %all-to-all-start.1 = ((bf16[4,1,24]{2,1,0:T(2,128)(2,1)}), bf16[4,1,24]{2,1,0:T(2,128)(2,1)S(1)}, u32[]{:S(2)}, u32[]{:S(2)}) async-start(bf16[4,1,24]{2,1,0:T(2,128)(2,1)} %all_to_all.15), calls=%async_computation.1 | async-start | bytes 4096 | tf_op jit(solution)/shard_map/all_to_all | solution.py:38
  35.4 4.0 %all-to-all-done.1 = bf16[4,1,24]{2,1,0:T(2,128)(2,1)S(1)} async-done(((bf16[4,1,24]{2,1,0:T(2,128)(2,1)}), bf16[4,1,24]{2,1,0:T(2,128)(2,1)S(1)}, u32[]{:S(2)}, u32[]{:S(2)}) %all-to-all-start.1) | async-done | bytes 224 | tf_op jit(solution)/shard_map/all_to_all | solution.py:38
  39.4 27.3 %all-gather = bf16[128,1,24]{2,1,0:T(2,128)(2,1)S(1)} all-gather(bf16[4,1,24]{2,1,0:T(2,128)(2,1)S(1)} %all-to-all-done.1), channel_id=2, replica_groups=mesh['expert'=4,'panel'=32] {'panel'}, dimensions={0}, use_global_device_ids=true | all-gather | bytes 6336 | tf_op jit(solution)/shard_map/all_gather | solution.py:43
  66.7 0.1 copy.29
  66.8 89.8 %all-gather.3.cloned.1.call-done = bf16[128,24,6144]{2,1,0:T(8,128)(2,1)} async-done(((bf16[4,24,6144]{2,1,0:T(8,128)(2,1)}), bf16[128,24,6144]{2,1,0:T(8,128)(2,1)}) %all-gather.3.cloned.1.call-update) | async-done | bytes 37748752 | tf_op jit(solution)/shard_map/all_gather | solution.py:40
  156.6 0.0 copy-start.1
  156.7 47.4 %copy.27 = bf16[128,24,6144]{0,2,1:T(8,128)(2,1)} copy(bf16[128,24,6144]{2,1,0:T(8,128)(2,1)} %all-gather.3.cloned.1.call-done) | data formatting | bytes 75497472 | tf_op jit(solution)/shard_map/all_gather | solution.py:40
  204.1 21.9 %bitcast_multiply_fusion = f32[2,192,6144]{2,1,0:T(8,128)} fusion(bf16[128,2,12,6144]{0,3,2,1:T(8,128)(2,1)} %bitcast.17, f32[128,2,12]{0,2,1:T(8,128)S(1)} %reshape.50, s32[]{:T(128)S(6)} %select_n.3), kind=kOutput, calls=%fused_computation.3 | convolution fusion | flops 7306739712 | bytes 48377860 | tf_op jit(solution)/shard_map/secu,secd->eud/dot_general | solution.py:50
  226.0 0.0 copy-done.1
  (1 shorter events, 0.0 us)
Async XLA Ops:
  6.5 2.2 copy-start
  6.5 150.1 %all-gather.3.cloned.1.call-start = ((), (), s32[]{:S(2)}) async-start(), calls=%async_computation.2 | async-start | bytes 38928384 | tf_op jit(solution)/shard_map/all_gather | solution.py:40
  32.2 7.2 %all-to-all-start.1 = ((bf16[4,1,24]{2,1,0:T(2,128)(2,1)}), bf16[4,1,24]{2,1,0:T(2,128)(2,1)S(1)}, u32[]{:S(2)}, u32[]{:S(2)}) async-start(bf16[4,1,24]{2,1,0:T(2,128)(2,1)} %all_to_all.15), calls=%async_computation.1 | async-start | bytes 4096 | tf_op jit(solution)/shard_map/all_to_all | solution.py:38
  156.6 69.4 %copy-start.1 = (bf16[32,6144]{1,0:T(8,128)(2,1)S(1)}, bf16[32,6144]{1,0:T(8,128)(2,1)}, u32[]{:S(2)}) copy-start(bf16[32,6144]{1,0:T(8,128)(2,1)} %param.3) | copy-start | bytes 1179652
Sparse Core Ops, SparseCore 0:
  30.8 125.8 all-gather.2
where the time goes:
time: 234 us; the launch traced here: 233 us
  waiting for transfers between devices  93.8 us (40%)
  local copies, waits for them, and re-layouts  49.3 us (21%)
  blocking collectives  48.7 us (21%)
  matrix products  22.6 us (10%)
  between operations  13.4 us (6%)
  starting transfers between devices  3.22 us (1%)
    all_gather x1, waiting for transfers between devices, per_device(): lax.all_gather(arrived_rows, 'panel', axis=0, tiled=True)  89.8 us
    all_gather x1, local copies, waits for them, and re-layouts, per_device(): lax.all_gather(arrived_rows, 'panel', axis=0, tiled=True)  47.4 us
    all_gather x1, blocking collectives, per_device(): lax.all_gather(arrived_weights, 'panel', axis=0, tiled=True)  27.3 us
    dot_general x1, matrix products, per_device(): jnp.einsum('secu,secd->eud', columns, scaled, preferred_element_type=jnp....  21.9 us
    all_to_all x1, blocking collectives, per_device(): lax.all_to_all(routed_rows, 'expert', split_axis=0, concat_axis=0, tiled=...  21.3 us
  transfers between devices with their start and end apart: 2, of which 2 were waited for; matrix products, arithmetic and copies ran while one was open for 0% of the time, Pallas kernels for 0%

commit v1 on v0

v1 whole, which is shorter than its diff:
```python
import jax
import jax.numpy as jnp
from jax import lax
from jax.sharding import PartitionSpec as P

EXPERTS = 8
CAP = 12


def per_device(tokens, routes, router_weights):
    count, width = tokens.shape
    groups = lax.axis_size("expert")
    panels = lax.axis_size("panel")
    quarter = width // groups
    panel_width = width // panels
    scaling = float(groups * panels * CAP) ** (-0.5)
    rounded = router_weights.astype(jnp.bfloat16)
    ids = jnp.arange(64, dtype=jnp.int32)[None, :]
    zero = jnp.zeros((), jnp.bfloat16)
    dense = jnp.where(routes[:, 0:1] == ids, rounded[:, 0:1], zero) + jnp.where(
        routes[:, 1:2] == ids, rounded[:, 1:2], zero
    )
    seed = lax.all_to_all(
        tokens.reshape(count, groups, quarter), "expert", split_axis=1, concat_axis=0, tiled=True
    ).reshape(groups * count, quarter)
    columns = lax.all_gather(seed, "panel", axis=0, tiled=True)
    rows = jnp.concatenate(
        [
            tokens.reshape(count, panels, panel_width),
            jnp.broadcast_to(dense[:, None, :], (count, panels, 64)),
        ],
        axis=2,
    )
    rows = lax.all_to_all(rows, "panel", split_axis=1, concat_axis=0, tiled=True)
    rows = rows.reshape(panels * count, panel_width + 64)
    rows = lax.all_gather(rows, "expert", axis=0, tiled=True)
    rows = rows.reshape(groups, panels, count, panel_width + 64).transpose(3, 1, 0, 2)
    rows = rows.reshape(panel_width + 64, -1)
    weights = rows[panel_width : panel_width + EXPERTS]
    scaled = (weights[:, None, :] * rows[None, :panel_width, :]).reshape(-1, rows.shape[1])
    blocks = jnp.dot(scaled, columns, preferred_element_type=jnp.float32) * scaling
    blocks = blocks.astype(jnp.bfloat16).reshape(groups, EXPERTS // groups, panel_width, quarter)
    blocks = lax.all_to_all(blocks, "expert", split_axis=0, concat_axis=0, tiled=True)
    return blocks.transpose(1, 2, 0, 3).reshape(-1, panel_width, width).astype(jnp.float32)


def solution(mesh):
    placed = (
        P(("expert", "panel"), None),
        P(("expert", "panel"), None),
        P(("expert", "panel"), None),
    )
    return jax.shard_map(
        per_device,
        mesh=mesh,
        in_specs=placed,
        out_specs=P("expert", "panel", None),
        check_vma=False,
    )
```

time: 234 us -> 222 us (0.949)
  blocking collectives: 48.7 us -> 90.3 us
  local copies, waits for them, and re-layouts: 49.3 us -> 13.6 us
  waiting for transfers between devices: 93.8 us -> 69.6 us
  other arithmetic: 1.81 us -> 9.06 us
  matrix products: 22.6 us -> 26 us
  starting transfers between devices: 3.22 us -> 0.04 us
    all_to_all x1 -> x3, blocking collectives: 21.3 us -> 90.3 us  [the longest x1 57.9 us: per_device(): lax.all_to_all(blocks, 'expert', split_axis=0, concat_axis=0, tiled=True)]
    all_gather x2 -> x0, local copies, waits for them, and re-layouts: 47.5 us -> none  [the longest x1 47.4 us: per_device(): lax.all_gather(arrived_rows, 'panel', axis=0, tiled=True)]
    all_gather x1 -> x0, blocking collectives: 27.3 us -> none  [per_device(): lax.all_gather(arrived_weights, 'panel', axis=0, tiled=True)]
    all_gather x1 -> x2, waiting for transfers between devices: 89.8 us -> 69.5 us  [the longest x1 51.5 us: per_device(): columns = lax.all_gather(seed, 'panel', axis=0, tiled=True)]
    mul x0 -> x1, other arithmetic: none -> 6.83 us  [per_device(): weights[:, None, :] * rows[None, :panel_width, :]]
    convert_element_type x1, local copies, waits for them, and re-layouts: 0.02 us -> 4.6 us  [per_device(): blocks.transpose(1, 2, 0, 3).reshape(-1, panel_width, width)]
    reshape x0 -> x3, local copies, waits for them, and re-layouts: none -> 4.48 us  [the longest x1 1.82 us: per_device(): rows.reshape(groups, panels, count, panel_width + 64).transpose(3, 1, 0, 2)]
    all_to_all x1 -> x0, waiting for transfers between devices: 3.99 us -> none  [per_device(): lax.all_to_all(routed_weights, 'expert', split_axis=0, concat_axis=0, til...]
  transfers between devices with their start and end apart: 2 -> 2, of which waited for: 2 -> 2; matrix products, arithmetic and copies ran while one was open for 0% -> 6% of each run, Pallas kernels for 0% -> 0%
where the time goes in v1:
time: 222 us
  blocking collectives  90.3 us (41%)
  waiting for transfers between devices  69.6 us (31%)
  matrix products  26 us (12%)
  local copies, waits for them, and re-layouts  13.6 us (6%)
  between operations  13.5 us (6%)
  other arithmetic  9.06 us (4%)
    all_to_all x1, blocking collectives, per_device(): lax.all_to_all(blocks, 'expert', split_axis=0, concat_axis=0, tiled=True)  57.9 us
    all_gather x1, waiting for transfers between devices, per_device(): columns = lax.all_gather(seed, 'panel', axis=0, tiled=True)  51.5 us
    dot_general x1, matrix products, per_device(): jnp.dot(scaled, columns, preferred_element_type=jnp.float32) * scaling  26 us
    all_to_all x1, blocking collectives, per_device(): lax.all_to_all(rows, 'panel', split_axis=1, concat_axis=0, tiled=True)  20 us
    all_gather x1, waiting for transfers between devices, per_device(): rows = lax.all_gather(rows, 'expert', axis=0, tiled=True)  18 us
    all_to_all x1, blocking collectives, per_device(): lax.all_to_all(tokens.reshape(count, groups, quarter), 'expert', split_ax...  12.3 us
    mul x1, other arithmetic, per_device(): weights[:, None, :] * rows[None, :panel_width, :]  6.83 us
    convert_element_type x1, local copies, waits for them, and re-layouts, per_device(): blocks.transpose(1, 2, 0, 3).reshape(-1, panel_width, width)  4.6 us
  transfers between devices with their start and end apart: 2, of which 2 were waited for; matrix products, arithmetic and copies ran while one was open for 6% of the time, Pallas kernels for 0%

profile of v1, /device:TPU:1, one launch (start us, length us, event | category | flops | bytes accessed | tf_op | source)
XLA Modules:
  0.0 222.1 jit_solution(15191602077753477741)
XLA Ops:
  6.5 0.0 all-gather.3.cloned.1.call-start
  6.5 0.7 convert_element_type.15
  7.2 0.8 slice_bitcast_fusion.3
  8.0 1.6 reshape.97
  9.6 0.1 fusion.3
  9.8 0.2 pad_maximum_fusion
  9.9 0.3 copy.15
  10.2 20.0 %all_to_all.35 = bf16[32,32,256]{2,0,1:T(8,128)(2,1)} all-to-all(bf16[32,32,256]{2,0,1:T(8,128)(2,1)S(1)} %copy.15), channel_id=1, replica_groups=mesh['expert'=4,'panel'=32] {'panel'}, dimensions={1} | all-to-all | bytes 1048576 | tf_op jit(solution)/shard_map/all_to_all | solution.py:34
  30.3 0.0 all-gather.3.cloned.1.call-update
  30.3 0.0 all-gather.5.cloned.1.call-start
  30.3 1.0 copy.27
  31.4 12.3 %all_to_all.36 = bf16[32,4,1536]{2,0,1:T(8,128)(2,1)} all-to-all(bf16[32,4,1536]{2,0,1:T(8,128)(2,1)S(1)} %bitcast.46), channel_id=1, replica_groups=mesh['expert'=4,'panel'=32] {'expert'}, dimensions={1} | all-to-all | bytes 786432 | tf_op jit(solution)/shard_map/all_to_all | solution.py:23
  43.7 0.0 all-gather.5.cloned.1.call-update
  43.7 18.0 %all-gather.3.cloned.1.call-done = bf16[4096,256]{1,0:T(8,128)(2,1)} async-done(((bf16[1024,256]{1,0:T(8,128)(2,1)}), bf16[4096,256]{1,0:T(8,128)(2,1)}) %all-gather.3.cloned.1.call-update) | async-done | bytes 2097168 | tf_op jit(solution)/shard_map/all_gather | solution.py:36
  61.7 1.8 copy.26
  63.6 0.4 slice.26
  64.0 0.3 copy.21
  64.3 2.7 %copy.18 = bf16[192,4096]{1,0:T(8,128)(2,1)} copy(bf16[192,4096]{0,1:T(8,128)(2,1)S(1)} %bitcast.38) | data formatting | bytes 3145728 | tf_op jit(solution)/shard_map/mul | solution.py:40
  67.0 6.8 %broadcast_multiply_fusion = bf16[8,192,4096]{2,1,0:T(8,128)(2,1)} fusion(bf16[192,4096]{1,0:T(8,128)(2,1)} %copy.18, bf16[8,4096]{1,0:T(8,128)(2,1)S(1)} %copy.21), kind=kLoop, calls=%fused_computation.3 | loop fusion | flops 6291456 | bytes 14221312 | tf_op jit(solution)/shard_map/mul | solution.py:40
  73.8 51.5 %all-gather.5.cloned.1.call-done = bf16[4096,1536]{1,0:T(8,128)(2,1)} async-done(((bf16[128,1536]{1,0:T(8,128)(2,1)}), bf16[4096,1536]{1,0:T(8,128)(2,1)}) %all-gather.5.cloned.1.call-update) | async-done | bytes 12582928 | tf_op jit(solution)/shard_map/all_gather | solution.py:26
  125.3 26.0 %fusion = bf16[1536,1536]{1,0:T(8,128)(2,1)S(1)} fusion(bf16[1536,4096]{1,0:T(8,128)(2,1)} %bitcast.39, bf16[4096,1536]{1,0:T(8,128)(2,1)} %all-gather.5.cloned.1.call-done), kind=kOutput, calls=%fused_computation.2 | convolution fusion | flops 19332071424 | bytes 29884416 | tf_op jit(solution)/shard_map/dot_general | solution.py:41
  151.4 57.9 %all_to_all.37 = bf16[4,2,192,1536]{3,2,1,0:T(8,128)(2,1)S(1)} all-to-all(bf16[4,2,192,1536]{3,2,1,0:T(8,128)(2,1)S(1)} %bitcast.40), channel_id=1, replica_groups=mesh['expert'=4,'panel'=32] {'expert'}, dimensions={0} | all-to-all | bytes 9437184 | tf_op jit(solution)/shard_map/all_to_all | solution.py:43
  209.3 1.3 convert_bitcast_fusion
  210.6 4.6 %copy.23 = f32[4,2,24,8,1536]{4,3,0,2,1:T(8,128)} copy(f32[4,2,24,8,1536]{4,3,2,1,0:T(8,128)S(1)} %convert_bitcast_fusion) | data formatting | bytes 18874368 | tf_op jit(solution)/shard_map/convert_element_type | solution.py:44
  (2 shorter events, 0.0 us)
Async XLA Ops:
  6.5 55.2 %all-gather.3.cloned.1.call-start = ((), (), s32[]{:S(2)}) async-start(), calls=%async_computation.3 | async-start | bytes 2621440 | tf_op jit(solution)/shard_map/all_gather | solution.py:36
  30.3 95.0 %all-gather.5.cloned.1.call-start = ((), (), s32[]{:S(2)}) async-start(), calls=%async_computation.4 | async-start | bytes 12976128 | tf_op jit(solution)/shard_map/all_gather | solution.py:26
Sparse Core Ops, SparseCore 0:
  30.4 31.2 all-gather.2
  64.0 61.3 all-gather.4

commit v2 on v1

v2 whole, which is shorter than its diff:
```python
import jax
import jax.numpy as jnp
from jax import lax
from jax.experimental import pallas as pl
from jax.experimental.pallas import tpu as pltpu
from jax.sharding import PartitionSpec as P

MESH = pl.DeviceIdType.MESH
Z, Y, X, C = 4, 4, 4, 2
EXPERTS = 8
OWN = EXPERTS // Z
CAP = 12
TOK = 32
WPAD = 128
TILE = 256
PIECES = ((0, 640), (640, 512), (1152, 512))
PLANE = [(dy, dx) for dy in range(Y) for dx in range(X) if (dy, dx) != (0, 0)]


def kernel(
    tok, routes, router_weights, out,
    cols, rows, rows_t, scaled, stage,
    own_sem, x1_s, x1_r, x2_s, x2_r, xd_s, xd_r, seed_s, seed_r,
    p1_s, p1_r, p2_s, p2_r, d_s, d_r, out_s, out_r, keep_sem,
):
    width = tok.shape[1]
    quarter = width // Z
    chip_rows = width // (Y * X)
    dev_rows = chip_rows // C
    scaling = float(Z * Y * X * C * CAP) ** -0.5
    z = lax.axis_index("expert")
    p = lax.axis_index("panel")
    y, x, c = p // (X * C), lax.rem(p // C, X), lax.rem(p, C)

    def at_z(dz):
        return (lax.rem(z + dz, Z), p)

    def at_plane(dy, dx):
        return (z, (lax.rem(y + dy, Y) * X + lax.rem(x + dx, X)) * C + c)

    sibling = (z, p + 1 - 2 * c)

    def remote(src, dst, send, recv, device):
        return pltpu.make_async_remote_copy(
            src_ref=src, dst_ref=dst, send_sem=send, recv_sem=recv, device_id=device, device_id_type=MESH
        )

    ids = lax.broadcasted_iota(jnp.int32, (TOK, WPAD), 1)
    chosen = routes[...]
    rounded = router_weights[...].astype(jnp.bfloat16).astype(jnp.float32)
    dense = jnp.where(ids == chosen[:, 0:1], rounded[:, 0:1], 0.0) + jnp.where(
        ids == chosen[:, 1:2], rounded[:, 1:2], 0.0
    )
    cols[z, y, x, c, :, 0:WPAD] = dense.astype(jnp.bfloat16)

    barrier = pltpu.get_barrier_semaphore()
    peers = [at_z(dz) for dz in range(1, Z)] + [at_plane(dy, dx) for dy, dx in PLANE] + [sibling]
    for peer in peers:
        pl.semaphore_signal(barrier, inc=1, device_id=peer, device_id_type=MESH)
    pl.semaphore_wait(barrier, len(peers))

    def own_columns(device_z, start, size):
        return pl.ds(pl.multiple_of(device_z * quarter + start, 128), size)

    def row_columns(chip):
        return pl.ds(pl.multiple_of(chip * chip_rows, 128), chip_rows)

    x1 = []
    for k, (dy, dx) in enumerate(PLANE):
        chip = lax.rem(y + dy, Y) * X + lax.rem(x + dx, X)
        x1.append(
            remote(tok.at[:, row_columns(chip)], rows.at[z, y, x, c], x1_s.at[k], x1_r.at[k], at_plane(dy, dx))
        )
    x2 = [
        remote(rows.at[z, :, :, c], rows.at[z, :, :, c], x2_s.at[k], x2_r.at[k], at_z(k + 1)) for k in range(Z - 1)
    ]
    xd = remote(rows.at[:, :, :, c], rows.at[:, :, :, c], xd_s, xd_r, sibling)
    seeds = []
    for q, (low, size) in enumerate(PIECES):
        start = max(low, WPAD)
        span = low + size - start
        here = []
        for k in range(Z - 1):
            there = at_z(k + 1)
            here.append(
                remote(
                    tok.at[:, own_columns(there[0], start - WPAD, span)],
                    cols.at[z, y, x, c, :, pl.ds(start, span)],
                    seed_s.at[q, k], seed_r.at[q, k], there,
                )
            )
        seeds.append(here)
    weight_seeds = [
        remote(
            cols.at[z, y, x, c, :, pl.ds(0, WPAD)], cols.at[z, y, x, c, :, pl.ds(0, WPAD)],
            seed_s.at[len(PIECES), k], seed_r.at[len(PIECES), k], at_z(k + 1),
        )
        for k in range(Z - 1)
    ]
    seeds[0] = seeds[0] + weight_seeds
    p1, p2, d = [], [], []
    for q, (low, size) in enumerate(PIECES):
        span = pl.ds(low, size)
        first, second = [], []
        for k in range(3):
            along_x, along_y = at_plane(0, k + 1), at_plane(k + 1, 0)
            a1 = cols.at[pl.ds(0, 2), y, x, c, :, span]
            b1 = cols.at[pl.ds(2, 2), y, x, c, :, span]
            first.append(remote(a1, a1, p1_s.at[q, 0, k], p1_r.at[q, 0, k], along_x))
            first.append(remote(b1, b1, p1_s.at[q, 1, k], p1_r.at[q, 1, k], along_y))
            a2 = cols.at[pl.ds(0, 2), y, :, c, :, span]
            b2 = cols.at[pl.ds(2, 2), :, x, c, :, span]
            second.append(remote(a2, a2, p2_s.at[q, 0, k], p2_r.at[q, 0, k], along_y))
            second.append(remote(b2, b2, p2_s.at[q, 1, k], p2_r.at[q, 1, k], along_x))
        p1.append(first)
        p2.append(second)
        both = cols.at[:, :, :, c, :, span]
        d.append(remote(both, both, d_s.at[q], d_r.at[q], sibling))

    own_rows = pltpu.make_async_copy(tok.at[:, row_columns(y * X + x)], rows.at[z, y, x, c], own_sem.at[0])
    own_cols = pltpu.make_async_copy(
        tok.at[:, own_columns(z, 0, quarter)], cols.at[z, y, x, c, :, pl.ds(WPAD, quarter)], own_sem.at[1]
    )
    own_rows.start()
    own_cols.start()
    for copy in x1:
        copy.start()
    for here in seeds:
        for copy in here:
            copy.start()
    own_cols.wait()
    own_rows.wait()
    for q in range(len(PIECES)):
        for copy in seeds[q]:
            copy.wait_recv()
        for copy in p1[q]:
            copy.start()
    for copy in x1:
        copy.wait_recv()
    for copy in x2:
        copy.start()
    for q in range(len(PIECES)):
        for copy in p1[q]:
            copy.wait_recv()
        for copy in p2[q]:
            copy.start()
    for copy in p2[0]:
        copy.wait_recv()
    d[0].start()
    for copy in x2:
        copy.wait_recv()
    xd.start()
    d[0].wait_recv()
    xd.wait_recv()

    def build(j, carry):
        z0, y0 = j // Y, lax.rem(j, Y)
        span = pl.ds(pl.multiple_of(j * 256, 256), 256)
        rows_t[...] = rows[z0, y0].reshape(256, chip_rows).astype(jnp.float32).T
        weights = cols[z0, y0, :, :, :, 0:WPAD].reshape(256, WPAD).astype(jnp.float32).T
        own = rows_t[pl.ds(pl.multiple_of(c * dev_rows, dev_rows), dev_rows), :]
        for e in range(EXPERTS):
            scaled[pl.ds(e * dev_rows, dev_rows), span] = (own * weights[e : e + 1, :]).astype(jnp.bfloat16)
        return carry

    lax.fori_loop(0, Z * Y, build, 0)

    sent, kept = [], []
    tile = 0
    for q, (low, size) in enumerate(PIECES):
        start = max(low, WPAD)
        for lane in range(start, low + size, TILE):
            if lane == start and q > 0:
                d[q].wait_recv()
            place = lane - WPAD
            for k in (2, 1, 3, 0):
                owner = lax.rem(z + k, Z)
                total = jnp.zeros((OWN * dev_rows, TILE), jnp.float32)
                for z0 in range(Z):
                    left = scaled[
                        pl.ds(pl.multiple_of(owner * OWN * dev_rows, OWN * dev_rows), OWN * dev_rows),
                        pl.ds(z0 * 1024, 1024),
                    ]
                    right = cols[z0, :, :, :, :, pl.ds(lane, TILE)].reshape(1024, TILE)
                    total = total + jnp.dot(left, right, preferred_element_type=jnp.float32)
                stage[owner, :, :, pl.ds(place, TILE)] = (
                    (total * scaling).astype(jnp.bfloat16).reshape(OWN, dev_rows, TILE)
                )
                source = stage.at[owner, :, :, pl.ds(place, TILE)]
                target = out.at[:, :, own_columns(z, place, TILE)]
                if k:
                    copy = remote(source, target, out_s.at[tile, k - 1], out_r.at[tile, k - 1], at_z(k))
                    sent.append(copy)
                else:
                    copy = pltpu.make_async_copy(source, target, keep_sem.at[tile])
                    kept.append(copy)
                copy.start()
            if lane == start and q + 1 < len(PIECES):
                for copy in p2[q + 1]:
                    copy.wait_recv()
                d[q + 1].start()
            tile += 1

    for copy in kept:
        copy.wait()
    for copy in sent:
        copy.wait_recv()
    done = x1 + x2 + [xd] + [copy for group in seeds + p1 + p2 for copy in group] + d + sent
    for copy in done:
        copy.wait_send()


def per_device(tokens, routes, router_weights):
    width = tokens.shape[1]
    quarter = width // Z
    chip_rows = width // (Y * X)
    dev_rows = chip_rows // C
    count = Z * Y * X * C * TOK
    pieces = len(PIECES)
    dma = pltpu.SemaphoreType.DMA
    blocks = pl.pallas_call(
        kernel,
        out_shape=jax.ShapeDtypeStruct((OWN, dev_rows, width), jnp.bfloat16),
        in_specs=[pl.BlockSpec(memory_space=pltpu.VMEM)] * 3,
        out_specs=pl.BlockSpec(memory_space=pl.ANY),
        scratch_shapes=[
            pltpu.VMEM((Z, Y, X, C, TOK, WPAD + quarter), jnp.bfloat16),
            pltpu.VMEM((Z, Y, X, C, TOK, chip_rows), jnp.bfloat16),
            pltpu.VMEM((chip_rows, 256), jnp.float32),
            pltpu.VMEM((EXPERTS * dev_rows, count), jnp.bfloat16),
            pltpu.VMEM((Z, OWN, dev_rows, quarter), jnp.bfloat16),
            dma((2,)),
            dma((len(PLANE),)), dma((len(PLANE),)),
            dma((Z - 1,)), dma((Z - 1,)),
            dma, dma,
            dma((pieces + 1, Z - 1)), dma((pieces + 1, Z - 1)),
            dma((pieces, 2, 3)), dma((pieces, 2, 3)),
            dma((pieces, 2, 3)), dma((pieces, 2, 3)),
            dma((pieces,)), dma((pieces,)),
            dma((quarter // TILE, Z - 1)), dma((quarter // TILE, Z - 1)),
            dma((quarter // TILE,)),
        ],
        compiler_params=pltpu.CompilerParams(
            collective_id=0, has_side_effects=True, vmem_limit_bytes=56 << 20
        ),
    )(tokens, routes, router_weights)
    return blocks.astype(jnp.float32)


def solution(mesh):
    placed = (
        P(("expert", "panel"), None),
        P(("expert", "panel"), None),
        P(("expert", "panel"), None),
    )
    return jax.shard_map(
        per_device,
        mesh=mesh,
        in_specs=placed,
        out_specs=P("expert", "panel", None),
        check_vma=False,
    )
```

time: 222 us -> 117 us (0.53)
  Pallas kernels: 0 us -> 107 us
  blocking collectives: 90.3 us -> 0 us
  waiting for transfers between devices: 69.6 us -> 0 us
  matrix products: 26 us -> 0 us
  between operations: 13.5 us -> 0.01 us
  local copies, waits for them, and re-layouts: 13.6 us -> 2.72 us
    pallas_call x0 -> x1, Pallas kernels: none -> 107 us  [per_device(): pl.pallas_call(kernel, out_shape=jax.ShapeDtypeStruct((OWN, dev_rows, wid...]
    all_to_all x3 -> x0, blocking collectives: 90.3 us -> none  [the longest x1 57.9 us: per_device(): lax.all_to_all(blocks, 'expert', split_axis=0, concat_axis=0, tiled=True)]
    all_gather x2 -> x0, waiting for transfers between devices: 69.5 us -> none  [the longest x1 51.5 us: per_device(): columns = lax.all_gather(seed, 'panel', axis=0, tiled=True)]
    dot_general x1 -> x0, matrix products: 26 us -> none  [per_device(): jnp.dot(scaled, columns, preferred_element_type=jnp.float32) * scaling]
    mul x1 -> x0, other arithmetic: 6.83 us -> none  [per_device(): weights[:, None, :] * rows[None, :panel_width, :]]
    convert_element_type x1, other arithmetic: 0.68 us -> 7.24 us  [per_device(): return blocks.astype(jnp.float32)]
    convert_element_type x1 -> x0, local copies, waits for them, and re-layouts: 4.6 us -> none  [per_device(): blocks.transpose(1, 2, 0, 3).reshape(-1, panel_width, width)]
    reshape x3 -> x0, local copies, waits for them, and re-layouts: 4.48 us -> none  [the longest x1 1.82 us: per_device(): rows.reshape(groups, panels, count, panel_width + 64).transpose(3, 1, 0, 2)]
  transfers between devices with their start and end apart: 2 -> 0, of which waited for: 2 -> 0; matrix products, arithmetic and copies ran while one was open for 6% -> 0% of each run, Pallas kernels for 0% -> 0%
where the time goes in v2:
time: 117 us
  Pallas kernels  107 us (91%)
  other arithmetic  7.24 us (6%)
  local copies, waits for them, and re-layouts  2.72 us (2%)
    pallas_call x1, Pallas kernels, per_device(): pl.pallas_call(kernel, out_shape=jax.ShapeDtypeStruct((OWN, dev_rows, wid...  107 us
    convert_element_type x1, other arithmetic, per_device(): return blocks.astype(jnp.float32)  7.24 us
    unnamed x2, local copies, waits for them, and re-layouts  2.72 us

profile of v2, /device:TPU:1, one launch (start us, length us, event | category | flops | bytes accessed | tf_op | source)
XLA Modules:
  0.0 116.9 jit_solution(18272524420383688220)
XLA Ops:
  0.0 1.4 %copy.4.routes = s32[32,2]{1,0:T(8,128)} copy(s32[32,2]{0,1:T(2,128)} %param.4) | data formatting | bytes 512 | tf_op args[1]
  1.4 1.4 %copy.5.router_weights = f32[32,2]{1,0:T(8,128)} copy(f32[32,2]{0,1:T(2,128)} %param.5) | data formatting | bytes 512 | tf_op args[2]
  2.7 106.9 %shard_map.37 = bf16[2,192,6144]{2,1,0:T(8,128)(2,1)} custom-call(bf16[32,6144]{1,0:T(8,128)(2,1)} %tok.1, s32[32,2]{1,0:T(8,128)} %copy.4.routes, f32[32,2]{1,0:T(8,128)} %copy.5.router_weights), custom_call_target="tpu_custom_call" | custom-call | tf_op jit(solution)/shard_map/pallas_call | solution.py:221
  109.7 7.2 %convert_element_type.3 = f32[2,192,6144]{2,1,0:T(8,128)} convert(bf16[2,192,6144]{2,1,0:T(8,128)(2,1)} %shard_map.37) | non-fusion elementwise | flops 2359296 | bytes 14155776 | tf_op jit(solution)/shard_map/convert_element_type | solution.py:247

commit v3 on v1

v3 whole, which is shorter than its diff:
```python
import jax
import jax.numpy as jnp
from jax import lax
from jax.experimental import pallas as pl
from jax.experimental.pallas import tpu as pltpu
from jax.sharding import PartitionSpec as P

MESH = pl.DeviceIdType.MESH
Z, Y, X, C = 4, 4, 4, 2
EXPERTS = 8
OWN = EXPERTS // Z
CAP = 12
TOK = 32
WPAD = 128
TILE = 256
COMMON = 1024
PIECES = ((0, 384), (384, 512), (896, 512), (1408, 512), (1920, 512))
PLANE = [(dy, dx) for dy in range(Y) for dx in range(X) if (dy, dx) != (0, 0)]
COPIES = 160
LOCALS = 16


def kernel(tok, routes, router_weights, out, cols, rows, rows_t, scaled, stage, mine, send, recv, local):
    width = tok.shape[1]
    part = (width - COMMON) // Z
    chip_rows = width // (Y * X)
    dev_rows = chip_rows // C
    scaling = float(Z * Y * X * C * CAP) ** -0.5
    z = lax.axis_index("expert")
    p = lax.axis_index("panel")
    y, x, c = p // (X * C), lax.rem(p // C, X), lax.rem(p, C)
    up_z, down_z = lax.rem(z + 1, Z), lax.rem(z + 3, Z)
    up_y, down_y = lax.rem(y + 1, Y), lax.rem(y + 3, Y)
    up_x, down_x = lax.rem(x + 1, X), lax.rem(x + 3, X)

    def at_z(dz):
        return (lax.rem(z + dz, Z), p)

    def at_plane(dy, dx):
        return (z, (lax.rem(y + dy, Y) * X + lax.rem(x + dx, X)) * C + c)

    sibling = (z, p + 1 - 2 * c)
    started, kept = [], []

    def push(src, dst, device):
        k = len(started)
        copy = pltpu.make_async_remote_copy(
            src_ref=src, dst_ref=dst, send_sem=send.at[k], recv_sem=recv.at[k], device_id=device, device_id_type=MESH
        )
        copy.start()
        started.append(copy)
        return copy

    def same(ref, device):
        return push(ref, ref, device)

    def keep(src, dst):
        copy = pltpu.make_async_copy(src, dst, local.at[len(kept)])
        copy.start()
        kept.append(copy)
        return copy

    def arrive(copies):
        for copy in copies:
            copy.wait_recv()

    ids = lax.broadcasted_iota(jnp.int32, (WPAD, TOK), 0)
    chosen = routes[...]
    rounded = router_weights[...].astype(jnp.bfloat16).astype(jnp.float32)
    dense = jnp.where(ids == chosen[0:1, :], rounded[0:1, :], 0.0) + jnp.where(
        ids == chosen[1:2, :], rounded[1:2, :], 0.0
    )
    cols[z, y, x, c, :, 0:WPAD] = dense.T.astype(jnp.bfloat16)

    barrier = pltpu.get_barrier_semaphore()
    peers = [at_z(dz) for dz in range(1, Z)] + [at_plane(dy, dx) for dy, dx in PLANE] + [sibling]
    for peer in peers:
        pl.semaphore_signal(barrier, inc=1, device_id=peer, device_id_type=MESH)
    pl.semaphore_wait(barrier, len(peers))

    def part_columns(device_z, start, size):
        return pl.ds(pl.multiple_of(COMMON + device_z * part + start, 128), size)

    def row_columns(chip):
        return pl.ds(pl.multiple_of(chip * chip_rows, 128), chip_rows)

    x1 = []
    for dy, dx in PLANE:
        chip = lax.rem(y + dy, Y) * X + lax.rem(x + dx, X)
        x1.append(push(tok.at[:, row_columns(chip)], rows.at[z, y, x, c], at_plane(dy, dx)))
    seeds = []
    for q, (low, size) in enumerate(PIECES):
        here = []
        start = max(low, WPAD)
        span = low + size - start
        for k in (1, 3, 2):
            there = at_z(k)
            if q == 0:
                here.append(same(cols.at[z, y, x, c, :, pl.ds(0, WPAD)], there))
            if start < WPAD + part:
                source = tok.at[:, part_columns(there[0], start - WPAD, span)]
            else:
                source = tok.at[:, pl.ds(start - WPAD - part, span)]
            here.append(push(source, cols.at[z, y, x, c, :, pl.ds(start, span)], there))
        seeds.append(here)
    keep(tok.at[:, row_columns(y * X + x)], rows.at[z, y, x, c])
    keep(tok.at[:, part_columns(z, 0, part)], cols.at[z, y, x, c, :, pl.ds(WPAD, part)])
    keep(tok.at[:, pl.ds(0, COMMON)], cols.at[z, y, x, c, :, pl.ds(WPAD + part, COMMON)])
    for copy in kept:
        copy.wait()
    kept_before = len(kept)

    p1, p2, f2, d = {}, {}, {}, {}

    def span_of(q):
        return pl.ds(*PIECES[q])

    def phase1(q):
        arrive(seeds[q])
        s = span_of(q)
        p1[q] = []
        for k in (1, 3, 2):
            p1[q].append(same(cols.at[pl.ds(0, 2), y, x, c, :, s], at_plane(0, k)))
            p1[q].append(same(cols.at[pl.ds(2, 2), y, x, c, :, s], at_plane(k, 0)))

    def phase2(q):
        arrive(p1[q])
        s = span_of(q)
        p2[q] = []
        for k in (1, 3):
            p2[q].append(same(cols.at[pl.ds(0, 2), y, :, c, :, s], at_plane(k, 0)))
            p2[q].append(same(cols.at[pl.ds(2, 2), :, x, c, :, s], at_plane(0, k)))

    def forward(q):
        arrive(p2[q])
        s = span_of(q)
        f2[q] = [
            same(cols.at[0, down_y, :, c, :, s], at_plane(1, 0)),
            same(cols.at[2, :, down_x, c, :, s], at_plane(0, 1)),
            same(cols.at[1, up_y, :, c, :, s], at_plane(3, 0)),
            same(cols.at[3, :, up_x, c, :, s], at_plane(0, 3)),
        ]

    def share(q):
        arrive(f2[q])
        d[q] = same(cols.at[:, :, :, c, :, span_of(q)], sibling)

    def half(block, h):
        return rows.at[block, pl.ds(2 * h, 2), :, c]

    phase1(0)
    phase1(1)
    arrive(x1)
    up = [same(half(z, 0), at_z(1)), same(half(z, 1), at_z(1))]
    down = [same(half(z, 1), at_z(3)), same(half(z, 0), at_z(3))]
    xd = [same(rows.at[z, :, :, c], sibling)]
    phase2(0)
    phase1(2)
    arrive([up[0], down[0]])
    far = [same(half(down_z, 0), at_z(1)), same(half(up_z, 1), at_z(3))]
    forward(0)
    phase2(1)
    arrive([up[1]])
    xd.append(same(rows.at[down_z, :, :, c], sibling))
    arrive([down[1]])
    xd.append(same(rows.at[up_z, :, :, c], sibling))
    phase1(3)
    share(0)
    forward(1)
    arrive(far)
    xd.append(same(rows.at[lax.rem(z + 2, Z), :, :, c], sibling))
    phase2(2)
    phase1(4)
    d[0].wait_recv()

    def build(z0, y0, carry):
        span = pl.ds(pl.multiple_of((z0 * Y + y0) * 256, 256), 256)
        rows_t[...] = rows[z0, y0].reshape(256, chip_rows).astype(jnp.float32).T
        weights = cols[z0, y0, :, :, :, 0:WPAD].reshape(256, WPAD).astype(jnp.float32).T
        own = rows_t[pl.ds(pl.multiple_of(c * dev_rows, dev_rows), dev_rows), :]
        for e in range(EXPERTS):
            scaled[pl.ds(e * dev_rows, dev_rows), span] = (own * weights[e : e + 1, :]).astype(jnp.bfloat16)
        return carry

    for k, block in enumerate((z, down_z, up_z, lax.rem(z + 2, Z))):
        xd[k].wait_recv()
        lax.fori_loop(0, Y, lambda y0, carry, block=block: build(block, y0, carry), 0)

    def product(owner, lane):
        total = jnp.zeros((OWN * dev_rows, TILE), jnp.float32)
        first = pl.multiple_of(owner * OWN * dev_rows, OWN * dev_rows)
        for z0 in range(Z):
            left = scaled[pl.ds(first, OWN * dev_rows), pl.ds(z0 * 1024, 1024)]
            right = cols[z0, :, :, :, :, pl.ds(lane, TILE)].reshape(1024, TILE)
            total = total + jnp.dot(left, right, preferred_element_type=jnp.float32)
        return (total * scaling).astype(jnp.bfloat16).reshape(OWN, dev_rows, TILE)

    tiles = []

    def split_tile(lane):
        place = lane - WPAD
        for k in (2, 1, 3, 0):
            owner = lax.rem(z + k, Z)
            stage[owner, :, :, pl.ds(place, TILE)] = product(owner, lane)
            source = stage.at[owner, :, :, pl.ds(place, TILE)]
            target = out.at[:, :, part_columns(z, place, TILE)]
            if k:
                tiles.append(push(source, target, at_z(k)))
            else:
                keep(source, target)

    def common_tile(lane):
        place = lane - WPAD - part
        mine[:, :, pl.ds(place, TILE)] = product(z, lane)
        keep(mine.at[:, :, pl.ds(place, TILE)], out.at[:, :, pl.ds(place, TILE)])

    split_tile(128)
    share(1)
    forward(2)
    phase2(3)
    d[1].wait_recv()
    split_tile(384)
    phase2(4)
    split_tile(640)
    share(2)
    forward(3)
    d[2].wait_recv()
    split_tile(896)
    share(3)
    forward(4)
    split_tile(1152)
    d[3].wait_recv()
    common_tile(1408)
    common_tile(1664)
    share(4)
    d[4].wait_recv()
    common_tile(1920)
    common_tile(2176)

    for copy in kept[kept_before:]:
        copy.wait()
    arrive(tiles)
    for copy in started:
        copy.wait_send()


def per_device(tokens, routes, router_weights):
    width = tokens.shape[1]
    part = (width - COMMON) // Z
    chip_rows = width // (Y * X)
    dev_rows = chip_rows // C
    count = Z * Y * X * C * TOK
    dma = pltpu.SemaphoreType.DMA
    blocks = pl.pallas_call(
        kernel,
        out_shape=jax.ShapeDtypeStruct((OWN, dev_rows, width), jnp.bfloat16),
        in_specs=[pl.BlockSpec(memory_space=pltpu.VMEM)] * 3,
        out_specs=pl.BlockSpec(memory_space=pl.ANY),
        scratch_shapes=[
            pltpu.VMEM((Z, Y, X, C, TOK, WPAD + part + COMMON), jnp.bfloat16),
            pltpu.VMEM((Z, Y, X, C, TOK, chip_rows), jnp.bfloat16),
            pltpu.VMEM((chip_rows, 256), jnp.float32),
            pltpu.VMEM((EXPERTS * dev_rows, count), jnp.bfloat16),
            pltpu.VMEM((Z, OWN, dev_rows, part), jnp.bfloat16),
            pltpu.VMEM((OWN, dev_rows, COMMON), jnp.bfloat16),
            dma((COPIES,)),
            dma((COPIES,)),
            dma((LOCALS,)),
        ],
        compiler_params=pltpu.CompilerParams(
            collective_id=0, has_side_effects=True, vmem_limit_bytes=56 << 20
        ),
    )(tokens, routes.T, router_weights.T)
    return blocks.astype(jnp.float32)


def solution(mesh):
    placed = (
        P(("expert", "panel"), None),
        P(("expert", "panel"), None),
        P(("expert", "panel"), None),
    )
    return jax.shard_map(
        per_device,
        mesh=mesh,
        in_specs=placed,
        out_specs=P("expert", "panel", None),
        check_vma=False,
    )
```

time: 222 us -> 104 us (0.47)
  Pallas kernels: 0 us -> 96.2 us
  blocking collectives: 90.3 us -> 0 us
  waiting for transfers between devices: 69.6 us -> 0 us
  matrix products: 26 us -> 0 us
  local copies, waits for them, and re-layouts: 13.6 us -> 0 us
  between operations: 13.5 us -> 0.01 us
    pallas_call x0 -> x1, Pallas kernels: none -> 96.2 us  [per_device(): pl.pallas_call(kernel, out_shape=jax.ShapeDtypeStruct((OWN, dev_rows, wid...]
    all_to_all x3 -> x0, blocking collectives: 90.3 us -> none  [the longest x1 57.9 us: per_device(): lax.all_to_all(blocks, 'expert', split_axis=0, concat_axis=0, tiled=True)]
    all_gather x2 -> x0, waiting for transfers between devices: 69.5 us -> none  [the longest x1 51.5 us: per_device(): columns = lax.all_gather(seed, 'panel', axis=0, tiled=True)]
    dot_general x1 -> x0, matrix products: 26 us -> none  [per_device(): jnp.dot(scaled, columns, preferred_element_type=jnp.float32) * scaling]
    mul x1 -> x0, other arithmetic: 6.83 us -> none  [per_device(): weights[:, None, :] * rows[None, :panel_width, :]]
    convert_element_type x1, other arithmetic: 0.68 us -> 7.24 us  [per_device(): return blocks.astype(jnp.float32)]
    convert_element_type x1 -> x0, local copies, waits for them, and re-layouts: 4.6 us -> none  [per_device(): blocks.transpose(1, 2, 0, 3).reshape(-1, panel_width, width)]
    reshape x3 -> x0, local copies, waits for them, and re-layouts: 4.48 us -> none  [the longest x1 1.82 us: per_device(): rows.reshape(groups, panels, count, panel_width + 64).transpose(3, 1, 0, 2)]
  transfers between devices with their start and end apart: 2 -> 0, of which waited for: 2 -> 0; matrix products, arithmetic and copies ran while one was open for 6% -> 0% of each run, Pallas kernels for 0% -> 0%
where the time goes in v3:
time: 104 us; the launch traced here: 103 us
  Pallas kernels  96.2 us (92%)
  other arithmetic  7.24 us (7%)
    pallas_call x1, Pallas kernels, per_device(): pl.pallas_call(kernel, out_shape=jax.ShapeDtypeStruct((OWN, dev_rows, wid...  96.2 us
    convert_element_type x1, other arithmetic, per_device(): return blocks.astype(jnp.float32)  7.24 us

profile of v3, /device:TPU:1, one launch (start us, length us, event | category | flops | bytes accessed | tf_op | source)
XLA Modules:
  0.0 103.5 jit_solution(1725416388128465243)
XLA Ops:
  0.0 96.2 %shard_map.37 = bf16[2,192,6144]{2,1,0:T(8,128)(2,1)} custom-call(bf16[32,6144]{1,0:T(8,128)(2,1)} %tok.1, s32[2,32]{1,0:T(2,128)} %bitcast.2, f32[2,32]{1,0:T(2,128)} %bitcast.3), custom_call_target="tpu_custom_call" | custom-call | tf_op jit(solution)/shard_map/pallas_call | solution.py:254
  96.2 7.2 %convert_element_type.3 = f32[2,192,6144]{2,1,0:T(8,128)} convert(bf16[2,192,6144]{2,1,0:T(8,128)(2,1)} %shard_map.37) | non-fusion elementwise | flops 2359296 | bytes 14155776 | tf_op jit(solution)/shard_map/convert_element_type | solution.py:274

commit v4 on v3

--- a/solution.py
+++ b/solution.py
@@ -13,16 +13,17 @@
 TOK = 32
 WPAD = 128
 TILE = 256
-COMMON = 1024
-PIECES = ((0, 384), (384, 512), (896, 512), (1408, 512), (1920, 512))
+FAR = 512
+PIECES = ((0, 384), (384, 512), (896, 512), (1408, 256), (1664, 512))
 PLANE = [(dy, dx) for dy in range(Y) for dx in range(X) if (dy, dx) != (0, 0)]
 COPIES = 160
-LOCALS = 16
-
-
-def kernel(tok, routes, router_weights, out, cols, rows, rows_t, scaled, stage, mine, send, recv, local):
+LOCALS = 4
+STRIP = 16
+
+
+def kernel(tok, routes, router_weights, out, cols, rows, rows_t, scaled, stage, send, recv, local):
     width = tok.shape[1]
-    part = (width - COMMON) // Z
+    part = width // Z
     chip_rows = width // (Y * X)
     dev_rows = chip_rows // C
     scaling = float(Z * Y * X * C * CAP) ** -0.5
@@ -30,8 +31,6 @@
     p = lax.axis_index("panel")
     y, x, c = p // (X * C), lax.rem(p // C, X), lax.rem(p, C)
     up_z, down_z = lax.rem(z + 1, Z), lax.rem(z + 3, Z)
-    up_y, down_y = lax.rem(y + 1, Y), lax.rem(y + 3, Y)
-    up_x, down_x = lax.rem(x + 1, X), lax.rem(x + 3, X)
 
     def at_z(dz):
         return (lax.rem(z + dz, Z), p)
@@ -79,18 +78,17 @@
     pl.semaphore_wait(barrier, len(peers))
 
     def part_columns(device_z, start, size):
-        return pl.ds(pl.multiple_of(COMMON + device_z * part + start, 128), size)
+        return pl.ds(pl.multiple_of(device_z * part + start, 128), size)
+
+    def far_columns(device_z, start, size):
+        return part_columns(lax.rem(device_z + 2, Z), part - FAR + start, size)
 
     def row_columns(chip):
         return pl.ds(pl.multiple_of(chip * chip_rows, 128), chip_rows)
 
-    x1 = []
-    for dy, dx in PLANE:
-        chip = lax.rem(y + dy, Y) * X + lax.rem(x + dx, X)
-        x1.append(push(tok.at[:, row_columns(chip)], rows.at[z, y, x, c], at_plane(dy, dx)))
-    seeds = []
-    for q, (low, size) in enumerate(PIECES):
+    def seed(q):
         here = []
+        low, size = PIECES[q]
         start = max(low, WPAD)
         span = low + size - start
         for k in (1, 3, 2):
@@ -100,17 +98,23 @@
             if start < WPAD + part:
                 source = tok.at[:, part_columns(there[0], start - WPAD, span)]
             else:
-                source = tok.at[:, pl.ds(start - WPAD - part, span)]
+                source = tok.at[:, far_columns(there[0], start - WPAD - part, span)]
             here.append(push(source, cols.at[z, y, x, c, :, pl.ds(start, span)], there))
-        seeds.append(here)
+        return here
+
+    seeds = [seed(0)]
+    x1 = []
+    for dy, dx in PLANE:
+        chip = lax.rem(y + dy, Y) * X + lax.rem(x + dx, X)
+        x1.append(push(tok.at[:, row_columns(chip)], rows.at[z, y, x, c], at_plane(dy, dx)))
+    seeds += [seed(q) for q in range(1, len(PIECES))]
     keep(tok.at[:, row_columns(y * X + x)], rows.at[z, y, x, c])
     keep(tok.at[:, part_columns(z, 0, part)], cols.at[z, y, x, c, :, pl.ds(WPAD, part)])
-    keep(tok.at[:, pl.ds(0, COMMON)], cols.at[z, y, x, c, :, pl.ds(WPAD + part, COMMON)])
+    keep(tok.at[:, far_columns(z, 0, FAR)], cols.at[z, y, x, c, :, pl.ds(WPAD + part, FAR)])
     for copy in kept:
         copy.wait()
-    kept_before = len(kept)
-
-    p1, p2, f2, d = {}, {}, {}, {}
+
+    p1, p2, d = {}, {}, {}
 
     def span_of(q):
         return pl.ds(*PIECES[q])
@@ -127,38 +131,27 @@
         arrive(p1[q])
         s = span_of(q)
         p2[q] = []
-        for k in (1, 3):
+        for k in (1, 3, 2):
             p2[q].append(same(cols.at[pl.ds(0, 2), y, :, c, :, s], at_plane(k, 0)))
             p2[q].append(same(cols.at[pl.ds(2, 2), :, x, c, :, s], at_plane(0, k)))
 
-    def forward(q):
+    def share(q):
         arrive(p2[q])
-        s = span_of(q)
-        f2[q] = [
-            same(cols.at[0, down_y, :, c, :, s], at_plane(1, 0)),
-            same(cols.at[2, :, down_x, c, :, s], at_plane(0, 1)),
-            same(cols.at[1, up_y, :, c, :, s], at_plane(3, 0)),
-            same(cols.at[3, :, up_x, c, :, s], at_plane(0, 3)),
-        ]
-
-    def share(q):
-        arrive(f2[q])
         d[q] = same(cols.at[:, :, :, c, :, span_of(q)], sibling)
 
     def half(block, h):
         return rows.at[block, pl.ds(2 * h, 2), :, c]
 
     phase1(0)
-    phase1(1)
     arrive(x1)
     up = [same(half(z, 0), at_z(1)), same(half(z, 1), at_z(1))]
     down = [same(half(z, 1), at_z(3)), same(half(z, 0), at_z(3))]
     xd = [same(rows.at[z, :, :, c], sibling)]
+    phase1(1)
     phase2(0)
     phase1(2)
     arrive([up[0], down[0]])
     far = [same(half(down_z, 0), at_z(1)), same(half(up_z, 1), at_z(3))]
-    forward(0)
     phase2(1)
     arrive([up[1]])
     xd.append(same(rows.at[down_z, :, :, c], sibling))
@@ -166,10 +159,9 @@
     xd.append(same(rows.at[up_z, :, :, c], sibling))
     phase1(3)
     share(0)
-    forward(1)
+    phase2(2)
     arrive(far)
     xd.append(same(rows.at[lax.rem(z + 2, Z), :, :, c], sibling))
-    phase2(2)
     phase1(4)
     d[0].wait_recv()
 
@@ -197,81 +189,91 @@
 
     tiles = []
 
-    def split_tile(lane):
+    def split_tile(lane, between):
         place = lane - WPAD
         for k in (2, 1, 3, 0):
+            if k == 2 and place >= part - FAR:
+                continue
             owner = lax.rem(z + k, Z)
-            stage[owner, :, :, pl.ds(place, TILE)] = product(owner, lane)
-            source = stage.at[owner, :, :, pl.ds(place, TILE)]
-            target = out.at[:, :, part_columns(z, place, TILE)]
+            target = part_columns(z, place, TILE)
             if k:
-                tiles.append(push(source, target, at_z(k)))
+                source = stage.at[k - 1, :, :, pl.ds(place, TILE)]
+                source[...] = product(owner, lane)
+                tiles.append(push(source, out.at[:, :, target], at_z(k)))
             else:
-                keep(source, target)
-
-    def common_tile(lane):
+                out[:, :, target] = product(owner, lane)
+            for step, q in between.get(k, ()):
+                step(q)
+
+    def far_tile(lane):
         place = lane - WPAD - part
-        mine[:, :, pl.ds(place, TILE)] = product(z, lane)
-        keep(mine.at[:, :, pl.ds(place, TILE)], out.at[:, :, pl.ds(place, TILE)])
-
-    split_tile(128)
-    share(1)
-    forward(2)
-    phase2(3)
+        out[:, :, far_columns(z, place, TILE)] = product(z, lane)
+
+    split_tile(128, {0: ((share, 1), (phase2, 3))})
     d[1].wait_recv()
-    split_tile(384)
-    phase2(4)
-    split_tile(640)
-    share(2)
-    forward(3)
+    split_tile(384, {})
+    split_tile(640, {1: ((share, 2), (phase2, 4))})
     d[2].wait_recv()
-    split_tile(896)
-    share(3)
-    forward(4)
-    split_tile(1152)
+    split_tile(896, {0: ((share, 3),)})
+    split_tile(1152, {})
     d[3].wait_recv()
-    common_tile(1408)
-    common_tile(1664)
+    split_tile(1408, {})
     share(4)
     d[4].wait_recv()
-    common_tile(1920)
-    common_tile(2176)
-
-    for copy in kept[kept_before:]:
-        copy.wait()
+    far_tile(1664)
+    far_tile(1920)
+
     arrive(tiles)
     for copy in started:
         copy.wait_send()
 
 
+def widen(blocks, out, wide, sem):
+    dev_rows = blocks.shape[1]
+    copies = []
+    for k in range(OWN * dev_rows // STRIP):
+        e, low = k * STRIP // dev_rows, k * STRIP % dev_rows
+        wide[k] = blocks[e, low : low + STRIP, :].astype(jnp.float32)
+        copies.append(pltpu.make_async_copy(wide.at[k], out.at[e, pl.ds(low, STRIP), :], sem.at[k]))
+        copies[-1].start()
+    for copy in copies:
+        copy.wait()
+
+
 def per_device(tokens, routes, router_weights):
     width = tokens.shape[1]
-    part = (width - COMMON) // Z
+    part = width // Z
     chip_rows = width // (Y * X)
     dev_rows = chip_rows // C
     count = Z * Y * X * C * TOK
     dma = pltpu.SemaphoreType.DMA
     blocks = pl.pallas_call(
         kernel,
-        out_shape=jax.ShapeDtypeStruct((OWN, dev_rows, width), jnp.bfloat16),
+        out_shape=pltpu.VMEM((OWN, dev_rows, width), jnp.bfloat16),
         in_specs=[pl.BlockSpec(memory_space=pltpu.VMEM)] * 3,
-        out_specs=pl.BlockSpec(memory_space=pl.ANY),
+        out_specs=pl.BlockSpec(memory_space=pltpu.VMEM),
         scratch_shapes=[
-            pltpu.VMEM((Z, Y, X, C, TOK, WPAD + part + COMMON), jnp.bfloat16),
+            pltpu.VMEM((Z, Y, X, C, TOK, WPAD + part + FAR), jnp.bfloat16),
             pltpu.VMEM((Z, Y, X, C, TOK, chip_rows), jnp.bfloat16),
             pltpu.VMEM((chip_rows, 256), jnp.float32),
             pltpu.VMEM((EXPERTS * dev_rows, count), jnp.bfloat16),
-            pltpu.VMEM((Z, OWN, dev_rows, part), jnp.bfloat16),
-            pltpu.VMEM((OWN, dev_rows, COMMON), jnp.bfloat16),
+            pltpu.VMEM((Z - 1, OWN, dev_rows, part), jnp.bfloat16),
             dma((COPIES,)),
             dma((COPIES,)),
             dma((LOCALS,)),
         ],
         compiler_params=pltpu.CompilerParams(
-            collective_id=0, has_side_effects=True, vmem_limit_bytes=56 << 20
+            collective_id=0, has_side_effects=True, vmem_limit_bytes=50 << 20
         ),
     )(tokens, routes.T, router_weights.T)
-    return blocks.astype(jnp.float32)
+    return pl.pallas_call(
+        widen,
+        out_shape=jax.ShapeDtypeStruct((OWN, dev_rows, width), jnp.float32),
+        in_specs=[pl.BlockSpec(memory_space=pltpu.VMEM)],
+        out_specs=pl.BlockSpec(memory_space=pl.ANY),
+        scratch_shapes=[pltpu.VMEM((OWN * dev_rows // STRIP, STRIP, width), jnp.float32), dma((OWN * dev_rows // STRIP,))],
+        compiler_params=pltpu.CompilerParams(vmem_limit_bytes=16 << 20),
+    )(blocks)
 
 
 def solution(mesh):

time: 104 us -> 95.8 us (0.921)
  other arithmetic: 7.24 us -> 0 us
    convert_element_type x1 -> x0, other arithmetic: 7.24 us -> none  [per_device(): return blocks.astype(jnp.float32)]
    pallas_call x1 -> x2, Pallas kernels: 96.2 us -> 95.5 us  [the longest x1 91.7 us: per_device(): pl.pallas_call(kernel, out_shape=pltpu.VMEM((OWN, dev_rows, width), jnp.b...]
where the time goes in v4:
time: 95.8 us; the launch traced here: 95.7 us
  Pallas kernels  95.5 us (100%)
    pallas_call x1, Pallas kernels, per_device(): pl.pallas_call(kernel, out_shape=pltpu.VMEM((OWN, dev_rows, width), jnp.b...  91.7 us
    pallas_call x1, Pallas kernels, per_device(): pl.pallas_call(widen, out_shape=jax.ShapeDtypeStruct((OWN, dev_rows, widt...  3.82 us

profile of v4, /device:TPU:1, one launch (start us, length us, event | category | flops | bytes accessed | tf_op | source)
XLA Modules:
  0.0 95.7 jit_solution(13500744943734495157)
XLA Ops:
  0.0 91.7 %shard_map.37.blocks = bf16[2,192,6144]{2,1,0:T(8,128)(2,1)S(1)} custom-call(bf16[32,6144]{1,0:T(8,128)(2,1)} %tok.1, s32[2,32]{1,0:T(2,128)} %bitcast.2, f32[2,32]{1,0:T(2,128)} %bitcast.3), custom_call_target="tpu_custom_call" | custom-call | tf_op jit(solution)/shard_map/pallas_call | solution.py:250
  91.7 3.8 %shard_map.38 = f32[2,192,6144]{2,1,0:T(8,128)} custom-call(bf16[2,192,6144]{2,1,0:T(8,128)(2,1)S(1)} %shard_map.37.blocks), custom_call_target="tpu_custom_call" | custom-call | tf_op jit(solution)/shard_map/pallas_call | solution.py:269

commit v5 on v4

--- a/solution.py
+++ b/solution.py
@@ -189,9 +189,9 @@
 
     tiles = []
 
-    def split_tile(lane, between):
+    def split_tile(lane, between, which=(2, 1, 3, 0)):
         place = lane - WPAD
-        for k in (2, 1, 3, 0):
+        for k in which:
             if k == 2 and place >= part - FAR:
                 continue
             owner = lax.rem(z + k, Z)
@@ -209,16 +209,20 @@
         place = lane - WPAD - part
         out[:, :, far_columns(z, place, TILE)] = product(z, lane)
 
-    split_tile(128, {0: ((share, 1), (phase2, 3))})
+    split_tile(128, {3: ((share, 1), (phase2, 3))}, (2, 1, 3))
     d[1].wait_recv()
-    split_tile(384, {})
-    split_tile(640, {1: ((share, 2), (phase2, 4))})
+    split_tile(384, {}, (2, 1, 3))
+    split_tile(640, {1: ((share, 2), (phase2, 4))}, (2, 1, 3))
+    split_tile(128, {}, (0,))
     d[2].wait_recv()
-    split_tile(896, {0: ((share, 3),)})
-    split_tile(1152, {})
+    split_tile(896, {3: ((share, 3),)}, (2, 1, 3))
+    split_tile(1152, {}, (2, 1, 3))
+    split_tile(384, {}, (0,))
     d[3].wait_recv()
-    split_tile(1408, {})
+    split_tile(1408, {}, (2, 1, 3))
     share(4)
+    for lane in (640, 896, 1152, 1408):
+        split_tile(lane, {}, (0,))
     d[4].wait_recv()
     far_tile(1664)
     far_tile(1920)

time: 95.8 us -> 94.8 us (0.990)
  no operation moved by 1% of the time
where the time goes in v5:
time: 94.8 us; the launch traced here: 94.7 us
  Pallas kernels  94.6 us (100%)
    pallas_call x1, Pallas kernels, per_device(): pl.pallas_call(kernel, out_shape=pltpu.VMEM((OWN, dev_rows, width), jnp.b...  90.7 us
    pallas_call x1, Pallas kernels, per_device(): pl.pallas_call(widen, out_shape=jax.ShapeDtypeStruct((OWN, dev_rows, widt...  3.82 us

profile of v5, /device:TPU:1, one launch (start us, length us, event | category | flops | bytes accessed | tf_op | source)
XLA Modules:
  0.0 94.7 jit_solution(9999779489584647319)
XLA Ops:
  0.0 90.7 %shard_map.37.blocks = bf16[2,192,6144]{2,1,0:T(8,128)(2,1)S(1)} custom-call(bf16[32,6144]{1,0:T(8,128)(2,1)} %tok.1, s32[2,32]{1,0:T(2,128)} %bitcast.2, f32[2,32]{1,0:T(2,128)} %bitcast.3), custom_call_target="tpu_custom_call" | custom-call | tf_op jit(solution)/shard_map/pallas_call | solution.py:254
  90.7 3.8 %shard_map.38 = f32[2,192,6144]{2,1,0:T(8,128)} custom-call(bf16[2,192,6144]{2,1,0:T(8,128)(2,1)S(1)} %shard_map.37.blocks), custom_call_target="tpu_custom_call" | custom-call | tf_op jit(solution)/shard_map/pallas_call | solution.py:273

commit v6 on v5

--- a/solution.py
+++ b/solution.py
@@ -102,11 +102,11 @@
             here.append(push(source, cols.at[z, y, x, c, :, pl.ds(start, span)], there))
         return here
 
-    seeds = [seed(0)]
     x1 = []
     for dy, dx in PLANE:
         chip = lax.rem(y + dy, Y) * X + lax.rem(x + dx, X)
         x1.append(push(tok.at[:, row_columns(chip)], rows.at[z, y, x, c], at_plane(dy, dx)))
+    seeds = [seed(0)]
     seeds += [seed(q) for q in range(1, len(PIECES))]
     keep(tok.at[:, row_columns(y * X + x)], rows.at[z, y, x, c])
     keep(tok.at[:, part_columns(z, 0, part)], cols.at[z, y, x, c, :, pl.ds(WPAD, part)])
@@ -254,7 +254,7 @@
     blocks = pl.pallas_call(
         kernel,
         out_shape=pltpu.VMEM((OWN, dev_rows, width), jnp.bfloat16),
-        in_specs=[pl.BlockSpec(memory_space=pltpu.VMEM)] * 3,
+        in_specs=[pl.BlockSpec(memory_space=pl.ANY)] + [pl.BlockSpec(memory_space=pltpu.VMEM)] * 2,
         out_specs=pl.BlockSpec(memory_space=pltpu.VMEM),
         scratch_shapes=[
             pltpu.VMEM((Z, Y, X, C, TOK, WPAD + part + FAR), jnp.bfloat16),

time: 94.8 us -> 94.8 us (level)
  no operation moved by 1% of the time
where the time goes in v6:
time: 94.8 us; the launch traced here: 94.6 us
  Pallas kernels  94.5 us (100%)
    pallas_call x1, Pallas kernels, per_device(): pl.pallas_call(kernel, out_shape=pltpu.VMEM((OWN, dev_rows, width), jnp.b...  90.6 us
    pallas_call x1, Pallas kernels, per_device(): pl.pallas_call(widen, out_shape=jax.ShapeDtypeStruct((OWN, dev_rows, widt...  3.82 us

profile of v6, /device:TPU:1, one launch (start us, length us, event | category | flops | bytes accessed | tf_op | source)
XLA Modules:
  0.0 94.6 jit_solution(13411436398168054527)
XLA Ops:
  0.0 90.6 %shard_map.37.blocks = bf16[2,192,6144]{2,1,0:T(8,128)(2,1)S(1)} custom-call(bf16[32,6144]{1,0:T(8,128)(2,1)} %tok.1, s32[2,32]{1,0:T(2,128)} %bitcast.2, f32[2,32]{1,0:T(2,128)} %bitcast.3), custom_call_target="tpu_custom_call" | custom-call | tf_op jit(solution)/shard_map/pallas_call | solution.py:254
  90.6 3.8 %shard_map.38 = f32[2,192,6144]{2,1,0:T(8,128)} custom-call(bf16[2,192,6144]{2,1,0:T(8,128)(2,1)S(1)} %shard_map.37.blocks), custom_call_target="tpu_custom_call" | custom-call | tf_op jit(solution)/shard_map/pallas_call | solution.py:273
